TPU v7x, 32 devices: a whole 2x2x4 slice. The times are simulated.
32 devices in a mesh: blk: 8 (over z, x), rep: 4 (over y, core).
Axes of the slice: x: 2, y: 2, z: 4, core: 2. Of those that a mesh axis runs over, the one named last changes fastest.
Arguments:
- a_blocks: bfloat16 [24, 8, 6, 128, 128], P('blk', None, None, None, 'rep'), may hold values from -0.5 to 0.5
- a_cols: int32 [24, 8, 6], P('blk'), may hold values from 0 to 111, as said below
- b_blocks: bfloat16 [896, 4, 3, 128, 128], P('blk', 'rep'), may hold values from -6 to 6
- b_cols: int32 [896, 4, 3], P('blk', 'rep'), may hold values from 0 to 223, as said below
- c_cols: int32 [24, 4, 4], P(None, 'rep'), may hold values from 0 to 223, as said below
Outputs:
- c_blocks: float32 [24, 4, 4, 128, 128], P('blk', 'rep')
Inputs may be any that keep to these rules, and one draw needn't show every extreme that they name: `a_cols`: within each block row and panel the 6 entries are distinct. `b_cols`: within each block row and tile the 3 entries are distinct. `c_cols`: within each block row and tile the 4 entries are distinct.
All inputs are finite; a program needn't handle non-finite values.
Results may differ from a plain program's by a relative error of at most 0.0003.
Values may be sent and summed in bfloat16 or wider, within the bound.
No kernel may reach another device: no remote copies, remote signals or barrier semaphores. Data moves between devices by JAX's collectives and lax.ppermute only.
A program may use at most 128 MiB of HBM per device.

v0:
```python
import math
import jax
import jax.numpy as jnp
from jax import lax
from jax.sharding import PartitionSpec as P


def select_blocks(chosen, chosen_cols, wanted):
    hits = chosen_cols[..., :, None] == wanted
    total = None
    for slot_t in range(chosen.shape[-3]):
        term = jnp.where(
            hits[..., slot_t, :, None, None],
            chosen[..., slot_t, None, :, :],
            jnp.zeros((), chosen.dtype),
        )
        total = term if total is None else total + term
    return total


def term_maker(slab, slab_cols, local_b, local_bcols, pattern):
    total_rows = slab.shape[0]
    slots = slab.shape[2]
    width = slab.shape[3]
    slab = slab.reshape(total_rows, slots, width, width)
    slab_cols = slab_cols.reshape(total_rows, slots)

    def partial_term(start, count):
        group = math.gcd(count, 2)

        def one_group(index):
            first = index * group
            left = lax.dynamic_slice_in_dim(slab, first, group, 0)
            where_k = lax.dynamic_slice_in_dim(slab_cols, first, group, 0)
            wanted = lax.dynamic_slice_in_dim(pattern, first, group, 0)
            chosen = jnp.take(local_b, where_k, axis=0)
            chosen_cols = jnp.take(local_bcols, where_k, axis=0)
            picked = select_blocks(chosen, chosen_cols, wanted[:, None, None, :])
            return jnp.einsum("isab,iscbd->icad", left, picked, preferred_element_type=jnp.float32)

        terms = lax.map(one_group, jnp.arange(count // group, dtype=jnp.int32))
        return terms.reshape(count, pattern.shape[1], width, width)

    return partial_term


def per_device(a_blocks, a_cols, b_blocks, b_cols, c_cols):
    own_rows = a_blocks.shape[0]
    local_b = b_blocks[:, 0]
    local_bcols = b_cols[:, 0]
    pattern = c_cols[:, 0]
    per_pattern = pattern.shape[1]
    routed, slab_cols = (
        lax.all_to_all(a_blocks, "blk", split_axis=1, concat_axis=0, tiled=True),
        lax.all_to_all(a_cols, "blk", split_axis=1, concat_axis=0, tiled=True),
    )
    slab = lax.all_gather(routed, "rep", axis=4, tiled=True)
    partial_term = term_maker(slab, slab_cols, local_b, local_bcols, pattern)
    mine = lax.psum_scatter(
        partial_term(jnp.int32(0), own_rows * lax.axis_size("blk")),
        "blk",
        scatter_dimension=0,
        tiled=True,
    )
    width = a_blocks.shape[3]
    return mine.reshape(own_rows, 1, per_pattern, width, width)


def solution(mesh):
    placed = (
        P("blk", None, None, None, "rep"),
        P("blk", None, None),
        P("blk", "rep", None, None, None),
        P("blk", "rep", None),
        P(None, "rep", None),
    )
    return jax.shard_map(
        per_device,
        mesh=mesh,
        in_specs=placed,
        out_specs=P("blk", "rep", None, None, None),
        check_vma=False,
    )
```

profile of v0, /device:TPU:0, one launch (start us, length us, event | category | flops | bytes accessed | tf_op | source)
XLA Modules:
  0.0 355.9 jit_solution(1189941406154972925)
XLA Ops:
  6.5 1.5 copy.32
  8.0 36.0 %all_to_all.33 = bf16[3,8,6,128,32]{3,4,2,0,1:T(8,128)(2,1)S(1)} all-to-all(bf16[3,8,6,128,32]{3,4,2,0,1:T(8,128)(2,1)S(1)} %copy.32), channel_id=1, replica_groups=mesh['blk'=8,'rep'=4] {'blk'}, dimensions={1} | all-to-all | bytes 2359296 | tf_op jit(solution)/shard_map/all_to_all | solution.py:54
  44.0 1.8 copy.33
  45.8 0.6 copy.29
  46.4 3.3 all-to-all-start
  50.0 6.2 %all-to-all-done = s32[3,8,6]{2,0,1:T(4,128)S(1)} async-done(((s32[3,8,6]{2,0,1:T(4,128)}), s32[3,8,6]{2,0,1:T(4,128)S(1)}, u32[]{:S(2)}, u32[]{:S(2)}) %all-to-all-start) | async-done | bytes 608 | tf_op jit(solution)/shard_map/all_to_all | solution.py:55
  56.3 25.8 %all-gather.2.cloned.1.call-done = bf16[24,1,6,128,128]{3,0,2,1,4:T(8,128)(2,1)} async-done(((bf16[24,1,6,128,32]{3,0,2,1,4:T(8,128)(2,1)}), bf16[24,1,6,128,128]{3,0,2,1,4:T(8,128)(2,1)}) %all-gather.2.cloned.1.call-update) | async-done | bytes 4718608 | tf_op jit(solution)/shard_map/all_gather | solution.py:57
  82.1 148.8 %while.10 = (s32[]{:T(128)}, f32[12,2,4,128,128]{4,3,2,1,0:T(8,128)}, s32[12]{0:T(128)S(1)}, s32[24,6]{1,0:T(8,128)S(1)}, s32[112,3]{1,0:T(8,128)S(1)}, /*index=...) while((s32[]{:T(128)}, ...), condition=%wide.region_1.2_spmd, body=%wide.region_0.1_spmd.sunk | while | flops 205849856 | bytes 15211487 | solution.py:41
  82.1 0.6 dynamic_slice.22
  84.3 4.9 %gather_fusion.1 = bf16[12,3,128,128]{3,2,1,0:T(8,128)(2,1)S(1)} fusion(bf16[112,3,128,128]{3,2,1,0:T(8,128)(2,1)} %get-tuple-element.191, s32[1024]{0:T(1024)S(1)} %pad_clamp_fusion.2), kind=kCustom, calls=%fused_computation.1.clone.1 | custom fusion | bytes 2359344 | tf_op jit(solution)/shard_map/while/body/eval_jaxpr/jit(_take)/gather | solution.py:36
  90.2 1.8 constant_dynamic-slice_fusion.5
  92.5 0.9 fusion.23
  93.6 0.8 constant_dynamic-update-slice_fusion.2
  94.5 0.6 dynamic_slice.22
  96.7 4.9 %gather_fusion.1 = bf16[12,3,128,128]{3,2,1,0:T(8,128)(2,1)S(1)} fusion(bf16[112,3,128,128]{3,2,1,0:T(8,128)(2,1)} %get-tuple-element.191, s32[1024]{0:T(1024)S(1)} %pad_clamp_fusion.2), kind=kCustom, calls=%fused_computation.1.clone.1 | custom fusion | bytes 2359344 | tf_op jit(solution)/shard_map/while/body/eval_jaxpr/jit(_take)/gather | solution.py:36
  102.6 1.8 constant_dynamic-slice_fusion.5
  104.9 0.9 fusion.23
  106.0 0.8 constant_dynamic-update-slice_fusion.2
  106.9 0.6 dynamic_slice.22
  109.1 4.9 %gather_fusion.1 = bf16[12,3,128,128]{3,2,1,0:T(8,128)(2,1)S(1)} fusion(bf16[112,3,128,128]{3,2,1,0:T(8,128)(2,1)} %get-tuple-element.191, s32[1024]{0:T(1024)S(1)} %pad_clamp_fusion.2), kind=kCustom, calls=%fused_computation.1.clone.1 | custom fusion | bytes 2359344 | tf_op jit(solution)/shard_map/while/body/eval_jaxpr/jit(_take)/gather | solution.py:36
  115.0 1.8 constant_dynamic-slice_fusion.5
  117.3 0.9 fusion.23
  118.4 0.9 constant_dynamic-update-slice_fusion.2
  119.3 0.6 dynamic_slice.22
  121.5 4.9 %gather_fusion.1 = bf16[12,3,128,128]{3,2,1,0:T(8,128)(2,1)S(1)} fusion(bf16[112,3,128,128]{3,2,1,0:T(8,128)(2,1)} %get-tuple-element.191, s32[1024]{0:T(1024)S(1)} %pad_clamp_fusion.2), kind=kCustom, calls=%fused_computation.1.clone.1 | custom fusion | bytes 2359344 | tf_op jit(solution)/shard_map/while/body/eval_jaxpr/jit(_take)/gather | solution.py:36
  127.4 1.8 constant_dynamic-slice_fusion.5
  129.7 0.9 fusion.23
  130.8 0.9 constant_dynamic-update-slice_fusion.2
  133.9 4.9 %gather_fusion.1 = bf16[12,3,128,128]{3,2,1,0:T(8,128)(2,1)S(1)} fusion(bf16[112,3,128,128]{3,2,1,0:T(8,128)(2,1)} %get-tuple-element.191, s32[1024]{0:T(1024)S(1)} %pad_clamp_fusion.2), kind=kCustom, calls=%fused_computation.1.clone.1 | custom fusion | bytes 2359344 | tf_op jit(solution)/shard_map/while/body/eval_jaxpr/jit(_take)/gather | solution.py:36
  139.8 1.8 constant_dynamic-slice_fusion.5
  142.1 0.9 fusion.23
  143.2 0.9 constant_dynamic-update-slice_fusion.2
  146.3 4.9 %gather_fusion.1 = bf16[12,3,128,128]{3,2,1,0:T(8,128)(2,1)S(1)} fusion(bf16[112,3,128,128]{3,2,1,0:T(8,128)(2,1)} %get-tuple-element.191, s32[1024]{0:T(1024)S(1)} %pad_clamp_fusion.2), kind=kCustom, calls=%fused_computation.1.clone.1 | custom fusion | bytes 2359344 | tf_op jit(solution)/shard_map/while/body/eval_jaxpr/jit(_take)/gather | solution.py:36
  152.2 1.8 constant_dynamic-slice_fusion.5
  154.5 0.9 fusion.23
  155.6 0.9 constant_dynamic-update-slice_fusion.2
  158.7 4.9 %gather_fusion.1 = bf16[12,3,128,128]{3,2,1,0:T(8,128)(2,1)S(1)} fusion(bf16[112,3,128,128]{3,2,1,0:T(8,128)(2,1)} %get-tuple-element.191, s32[1024]{0:T(1024)S(1)} %pad_clamp_fusion.2), kind=kCustom, calls=%fused_computation.1.clone.1 | custom fusion | bytes 2359344 | tf_op jit(solution)/shard_map/while/body/eval_jaxpr/jit(_take)/gather | solution.py:36
  164.6 1.8 constant_dynamic-slice_fusion.5
  166.9 0.9 fusion.23
  168.0 0.9 constant_dynamic-update-slice_fusion.2
  168.9 0.6 dynamic_slice.22
  171.1 4.9 %gather_fusion.1 = bf16[12,3,128,128]{3,2,1,0:T(8,128)(2,1)S(1)} fusion(bf16[112,3,128,128]{3,2,1,0:T(8,128)(2,1)} %get-tuple-element.191, s32[1024]{0:T(1024)S(1)} %pad_clamp_fusion.2), kind=kCustom, calls=%fused_computation.1.clone.1 | custom fusion | bytes 2359344 | tf_op jit(solution)/shard_map/while/body/eval_jaxpr/jit(_take)/gather | solution.py:36
  177.0 1.8 constant_dynamic-slice_fusion.5
  179.3 0.9 fusion.23
  180.4 0.8 constant_dynamic-update-slice_fusion.2
  181.3 0.6 dynamic_slice.22
  183.5 4.9 %gather_fusion.1 = bf16[12,3,128,128]{3,2,1,0:T(8,128)(2,1)S(1)} fusion(bf16[112,3,128,128]{3,2,1,0:T(8,128)(2,1)} %get-tuple-element.191, s32[1024]{0:T(1024)S(1)} %pad_clamp_fusion.2), kind=kCustom, calls=%fused_computation.1.clone.1 | custom fusion | bytes 2359344 | tf_op jit(solution)/shard_map/while/body/eval_jaxpr/jit(_take)/gather | solution.py:36
  189.4 1.8 constant_dynamic-slice_fusion.5
  191.7 0.9 fusion.23
  192.8 0.8 constant_dynamic-update-slice_fusion.2
  193.7 0.6 dynamic_slice.22
  195.8 4.9 %gather_fusion.1 = bf16[12,3,128,128]{3,2,1,0:T(8,128)(2,1)S(1)} fusion(bf16[112,3,128,128]{3,2,1,0:T(8,128)(2,1)} %get-tuple-element.191, s32[1024]{0:T(1024)S(1)} %pad_clamp_fusion.2), kind=kCustom, calls=%fused_computation.1.clone.1 | custom fusion | bytes 2359344 | tf_op jit(solution)/shard_map/while/body/eval_jaxpr/jit(_take)/gather | solution.py:36
  201.8 1.8 constant_dynamic-slice_fusion.5
  204.1 0.9 fusion.23
  205.2 0.8 constant_dynamic-update-slice_fusion.2
  208.2 4.9 %gather_fusion.1 = bf16[12,3,128,128]{3,2,1,0:T(8,128)(2,1)S(1)} fusion(bf16[112,3,128,128]{3,2,1,0:T(8,128)(2,1)} %get-tuple-element.191, s32[1024]{0:T(1024)S(1)} %pad_clamp_fusion.2), kind=kCustom, calls=%fused_computation.1.clone.1 | custom fusion | bytes 2359344 | tf_op jit(solution)/shard_map/while/body/eval_jaxpr/jit(_take)/gather | solution.py:36
  214.1 1.8 constant_dynamic-slice_fusion.5
  216.5 0.9 fusion.23
  217.6 0.9 constant_dynamic-update-slice_fusion.2
  220.7 4.9 %gather_fusion.1 = bf16[12,3,128,128]{3,2,1,0:T(8,128)(2,1)S(1)} fusion(bf16[112,3,128,128]{3,2,1,0:T(8,128)(2,1)} %get-tuple-element.191, s32[1024]{0:T(1024)S(1)} %pad_clamp_fusion.2), kind=kCustom, calls=%fused_computation.1.clone.1 | custom fusion | bytes 2359344 | tf_op jit(solution)/shard_map/while/body/eval_jaxpr/jit(_take)/gather | solution.py:36
  226.6 1.8 constant_dynamic-slice_fusion.5
  228.9 0.9 fusion.23
  230.0 0.8 constant_dynamic-update-slice_fusion.2
  230.9 118.2 %reduce-scatter.2.cloned.1.call-done = f32[3,4,128,128]{3,2,1,0:T(8,128)} async-done(((f32[24,4,128,128]{3,2,1,0:T(8,128)}), f32[3,4,128,128]{3,2,1,0:T(8,128)}) %reduce-scatter.2.cloned.1.call-update) | async-done | bytes 786448 | tf_op jit(solution)/shard_map/reduce_scatter | solution.py:59
  (224 shorter events, 34.2 us)
Async XLA Ops:
  6.5 75.6 %all-gather.2.cloned.1.call-start = ((), (), s32[]{:S(2)}) async-start(), calls=%async_computation.3 | async-start | bytes 5898240 | tf_op jit(solution)/shard_map/all_gather | solution.py:57
  44.0 1.8 copy-start
  44.0 5.8 %copy-start.2 = (s32[112,1,3]{0,1,2:T(1,128)S(1)}, s32[112,1,3]{0,1,2:T(1,128)}, u32[]{:S(2)}) copy-start(s32[112,1,3]{0,1,2:T(1,128)} %param.10) | copy-start | bytes 4036
  44.0 5.9 %copy-start.1 = (s32[24,1,4]{0,2,1:T(4,128)S(1)}, s32[24,1,4]{0,2,1:T(4,128)}, u32[]{:S(2)}) copy-start(s32[24,1,4]{0,2,1:T(4,128)} %param.11) | copy-start | bytes 1156
  46.4 9.9 %all-to-all-start = ((s32[3,8,6]{2,0,1:T(4,128)}), s32[3,8,6]{2,0,1:T(4,128)S(1)}, u32[]{:S(2)}, u32[]{:S(2)}) async-start(s32[3,8,6]{2,0,1:T(4,128)} %copy.29), calls=%async_computation | async-start | bytes 32768 | tf_op jit(solution)/shard_map/all_to_all | solution.py:55
  49.8 299.3 %reduce-scatter.2.cloned.1.call-start = ((), (), s32[]{:S(2)}) async-start(), calls=%async_computation.4 | async-start | bytes 7077888 | tf_op jit(solution)/shard_map/reduce_scatter | solution.py:59
Sparse Core Ops, SparseCore 0:
  45.9 36.1 all-gather.1
  231.0 118.0 reduce-scatter.1
where the time goes:
time: 357 us; the launch traced here: 356 us
  waiting for transfers between devices  150 us (42%)
  local copies, waits for them, and re-layouts  130 us (36%)
  blocking collectives  36 us (10%)
  between operations  13.4 us (4%)
  matrix products  10.9 us (3%)
  loops' own time  8.92 us (2%)
    reduce_scatter x1, waiting for transfers between devices, per_device(): lax.psum_scatter(partial_term(jnp.int32(0), own_rows * lax.axis_size('blk...  118 us
    gather x12, local copies, waits for them, and re-layouts, one_group(): chosen = jnp.take(local_b, where_k, axis=0)  58.8 us
    all_to_all x1, blocking collectives, per_device(): lax.all_to_all(a_blocks, 'blk', split_axis=1, concat_axis=0, tiled=True)  36 us
    dynamic_slice x24, local copies, waits for them, and re-layouts, one_group(): left = lax.dynamic_slice_in_dim(slab, first, group, 0)  27.7 us
    all_gather x1, waiting for transfers between devices, per_device(): slab = lax.all_gather(routed, 'rep', axis=4, tiled=True)  25.8 us
    dynamic_update_slice x24, local copies, waits for them, and re-layouts, partial_term(): terms = lax.map(one_group, jnp.arange(count // group, dtype=jnp.int32))  12.6 us
    dot_general x12, matrix products, one_group(): jnp.einsum('isab,iscbd->icad', left, picked, preferred_element_type=jnp.f...  10.9 us
    broadcast_in_dim x60, local copies, waits for them, and re-layouts, select_blocks(): jnp.where(hits[..., slot_t, :, None, None], chosen[..., slot_t, None, :,...  9.59 us
  transfers between devices with their start and end apart: 3, of which 3 were waited for; matrix products, arithmetic and copies ran while one was open for 0% of the time, Pallas kernels for 0%

commit v1 on v0

--- a/solution.py
+++ b/solution.py
@@ -3,6 +3,18 @@
 import jax.numpy as jnp
 from jax import lax
 from jax.sharding import PartitionSpec as P
+
+
+def gather_by_bits(array, axis, dim):
+    ways, here = (lax.axis_size(axis), lax.axis_index(axis))
+    grown, reach = (array, 1)
+    while reach < ways:
+        theirs = lax.ppermute(grown, axis, [(d, d ^ reach) for d in range(ways)])
+        mine_first = jnp.concatenate([grown, theirs], axis=dim)
+        theirs_first = jnp.concatenate([theirs, grown], axis=dim)
+        grown = jnp.where(here & reach == 0, mine_first, theirs_first)
+        reach = 2 * reach
+    return grown
 
 
 def select_blocks(chosen, chosen_cols, wanted):
@@ -54,7 +66,7 @@
         lax.all_to_all(a_blocks, "blk", split_axis=1, concat_axis=0, tiled=True),
         lax.all_to_all(a_cols, "blk", split_axis=1, concat_axis=0, tiled=True),
     )
-    slab = lax.all_gather(routed, "rep", axis=4, tiled=True)
+    slab = gather_by_bits(routed, "rep", 4)
     partial_term = term_maker(slab, slab_cols, local_b, local_bcols, pattern)
     mine = lax.psum_scatter(
         partial_term(jnp.int32(0), own_rows * lax.axis_size("blk")),

time: 357 us -> 363 us (1.017)
  local copies, waits for them, and re-layouts: 130 us -> 99.8 us
  waiting for transfers between devices: 150 us -> 167 us
  other arithmetic: 3.44 us -> 12.7 us
  matrix products: 10.9 us -> 19.5 us
    ppermute x0 -> x2, waiting for transfers between devices: none -> 43.7 us  [gather_by_bits(): theirs = lax.ppermute(grown, axis, [(d, d ^ reach) for d in range(ways)])]
    dynamic_slice x24 -> x0, local copies, waits for them, and re-layouts: 27.7 us -> none  [one_group(): left = lax.dynamic_slice_in_dim(slab, first, group, 0)]
    all_gather x1 -> x0, waiting for transfers between devices: 25.8 us -> none  [per_device(): slab = lax.all_gather(routed, 'rep', axis=4, tiled=True)]
    select_n x0 -> x3, other arithmetic: none -> 9.24 us  [gather_by_bits(): grown = jnp.where(here & reach == 0, mine_first, theirs_first)]
    dot_general x12, matrix products: 10.9 us -> 19.5 us  [one_group(): jnp.einsum('isab,iscbd->icad', left, picked, preferred_element_type=jnp.f...]
  transfers between devices with their start and end apart: 3 -> 4, of which waited for: 3 -> 4; matrix products, arithmetic and copies ran while one was open for 0% -> 0% of each run, Pallas kernels for 0% -> 0%
where the time goes in v1:
time: 363 us; the launch traced here: 362 us
  waiting for transfers between devices  167 us (46%)
  local copies, waits for them, and re-layouts  99.8 us (27%)
  blocking collectives  36 us (10%)
  matrix products  19.5 us (5%)
  between operations  13.5 us (4%)
  other arithmetic  12.7 us (3%)
  loops' own time  8.72 us (2%)
  starting transfers between devices  4.9 us (1%)
    reduce_scatter x1, waiting for transfers between devices, per_device(): lax.psum_scatter(partial_term(jnp.int32(0), own_rows * lax.axis_size('blk...  117 us
    gather x12, local copies, waits for them, and re-layouts, one_group(): chosen = jnp.take(local_b, where_k, axis=0)  58.8 us
    ppermute x2, waiting for transfers between devices, gather_by_bits(): theirs = lax.ppermute(grown, axis, [(d, d ^ reach) for d in range(ways)])  43.7 us
    all_to_all x1, blocking collectives, per_device(): lax.all_to_all(a_blocks, 'blk', split_axis=1, concat_axis=0, tiled=True)  36 us
    dot_general x12, matrix products, one_group(): jnp.einsum('isab,iscbd->icad', left, picked, preferred_element_type=jnp.f...  19.5 us
    dynamic_update_slice x24, local copies, waits for them, and re-layouts, partial_term(): terms = lax.map(one_group, jnp.arange(count // group, dtype=jnp.int32))  12.5 us
    broadcast_in_dim x60, local copies, waits for them, and re-layouts, select_blocks(): jnp.where(hits[..., slot_t, :, None, None], chosen[..., slot_t, None, :,...  9.32 us
    select_n x3, other arithmetic, gather_by_bits(): grown = jnp.where(here & reach == 0, mine_first, theirs_first)  9.24 us
  transfers between devices with their start and end apart: 4, of which 4 were waited for; matrix products, arithmetic and copies ran while one was open for 0% of the time, Pallas kernels for 0%

profile of v1, /device:TPU:0, one launch (start us, length us, event | category | flops | bytes accessed | tf_op | source)
XLA Modules:
  0.0 361.9 jit_solution(17109297668415567814)
XLA Ops:
  6.5 1.5 copy.34
  8.0 36.0 %all_to_all.33 = bf16[3,8,6,128,32]{3,4,2,0,1:T(8,128)(2,1)S(1)} all-to-all(bf16[3,8,6,128,32]{3,4,2,0,1:T(8,128)(2,1)S(1)} %copy.34), channel_id=1, replica_groups=mesh['blk'=8,'rep'=4] {'blk'}, dimensions={1} | all-to-all | bytes 2359296 | tf_op jit(solution)/shard_map/all_to_all | solution.py:66
  44.0 2.8 collective-permute-done
  46.8 1.9 maximum_select_fusion.2
  48.8 1.5 collective-permute-start.1
  50.3 0.6 copy.31
  50.9 3.3 all-to-all-start
  54.5 6.2 %all-to-all-done = s32[3,8,6]{2,0,1:T(4,128)S(1)} async-done(((s32[3,8,6]{2,0,1:T(4,128)}), s32[3,8,6]{2,0,1:T(4,128)S(1)}, u32[]{:S(2)}, u32[]{:S(2)}) %all-to-all-start) | async-done | bytes 608 | tf_op jit(solution)/shard_map/all_to_all | solution.py:67
  60.8 0.7 maximum_select_fusion.1
  61.5 40.9 %collective-permute-done.1 = bf16[24,1,6,128,64]{3,4,2,1,0:T(8,128)(2,1)} collective-permute-done((bf16[24,1,6,128,64]{3,4,2,1,0:T(8,128)(2,1)}, bf16[24,1,6,128,64]{3,4,2,1,0:T(8,128)(2,1)}, u32[]{:S(2)}, u32[]{:S(2)}) %collective-permute-start.1) | collective-permute-done | bytes 2359328 | tf_op jit(solution)/shard_map/ppermute | solution.py:12
  102.4 6.6 %maximum_select_fusion = bf16[24,6,128,128]{2,3,1,0:T(8,128)(2,1)} fusion(bf16[24,6,128,64]{2,3,1,0:T(8,128)(2,1)} %bitcast.30, bf16[24,6,128,64]{2,3,1,0:T(8,128)(2,1)S(1)} %maximum_select_fusion.1, pred[]{:T(512)S(6)} %eq.19), kind=kLoop, calls=%fused_computation.34 | loop fusion | flops 21233664 | bytes 9437185 | tf_op jit(solution)/shard_map/jit(_where)/select_n | solution.py:15
  109.0 129.2 %while.10 = (s32[]{:T(128)}, f32[12,2,4,128,128]{4,3,2,1,0:T(8,128)}, s32[12]{0:T(128)S(1)}, s32[24,6]{1,0:T(8,128)S(1)}, s32[112,3]{1,0:T(8,128)S(1)}, /*index=...) while((s32[]{:T(128)}, ...), condition=%wide.region_1.2_spmd, body=%wide.region_0.1_spmd.sunk | while | flops 205849856 | bytes 13638623 | solution.py:53
  109.0 0.6 dynamic_slice.25
  110.3 0.6 gather_fusion
  111.2 4.9 %gather_fusion.1 = bf16[12,3,128,128]{3,2,1,0:T(8,128)(2,1)S(1)} fusion(bf16[112,3,128,128]{3,2,1,0:T(8,128)(2,1)} %get-tuple-element.191, s32[1024]{0:T(1024)S(1)} %pad_clamp_fusion.2), kind=kCustom, calls=%fused_computation.1.clone.1 | custom fusion | bytes 2359344 | tf_op jit(solution)/shard_map/while/body/eval_jaxpr/jit(_take)/gather | solution.py:48
  117.1 1.6 fusion.25
  118.9 0.8 constant_dynamic-update-slice_fusion.2
  119.7 0.6 dynamic_slice.25
  121.1 0.6 gather_fusion
  121.9 4.9 %gather_fusion.1 = bf16[12,3,128,128]{3,2,1,0:T(8,128)(2,1)S(1)} fusion(bf16[112,3,128,128]{3,2,1,0:T(8,128)(2,1)} %get-tuple-element.191, s32[1024]{0:T(1024)S(1)} %pad_clamp_fusion.2), kind=kCustom, calls=%fused_computation.1.clone.1 | custom fusion | bytes 2359344 | tf_op jit(solution)/shard_map/while/body/eval_jaxpr/jit(_take)/gather | solution.py:48
  127.8 1.6 fusion.25
  129.6 0.8 constant_dynamic-update-slice_fusion.2
  130.5 0.6 dynamic_slice.25
  132.7 4.9 %gather_fusion.1 = bf16[12,3,128,128]{3,2,1,0:T(8,128)(2,1)S(1)} fusion(bf16[112,3,128,128]{3,2,1,0:T(8,128)(2,1)} %get-tuple-element.191, s32[1024]{0:T(1024)S(1)} %pad_clamp_fusion.2), kind=kCustom, calls=%fused_computation.1.clone.1 | custom fusion | bytes 2359344 | tf_op jit(solution)/shard_map/while/body/eval_jaxpr/jit(_take)/gather | solution.py:48
  138.6 1.6 fusion.25
  140.4 0.9 constant_dynamic-update-slice_fusion.2
  141.3 0.6 dynamic_slice.25
  142.6 0.6 gather_fusion
  143.4 4.9 %gather_fusion.1 = bf16[12,3,128,128]{3,2,1,0:T(8,128)(2,1)S(1)} fusion(bf16[112,3,128,128]{3,2,1,0:T(8,128)(2,1)} %get-tuple-element.191, s32[1024]{0:T(1024)S(1)} %pad_clamp_fusion.2), kind=kCustom, calls=%fused_computation.1.clone.1 | custom fusion | bytes 2359344 | tf_op jit(solution)/shard_map/while/body/eval_jaxpr/jit(_take)/gather | solution.py:48
  149.3 1.6 fusion.25
  151.2 0.8 constant_dynamic-update-slice_fusion.2
  152.0 0.6 dynamic_slice.25
  154.2 4.9 %gather_fusion.1 = bf16[12,3,128,128]{3,2,1,0:T(8,128)(2,1)S(1)} fusion(bf16[112,3,128,128]{3,2,1,0:T(8,128)(2,1)} %get-tuple-element.191, s32[1024]{0:T(1024)S(1)} %pad_clamp_fusion.2), kind=kCustom, calls=%fused_computation.1.clone.1 | custom fusion | bytes 2359344 | tf_op jit(solution)/shard_map/while/body/eval_jaxpr/jit(_take)/gather | solution.py:48
  160.1 1.6 fusion.25
  161.9 0.8 constant_dynamic-update-slice_fusion.2
  162.8 0.6 dynamic_slice.25
  165.0 4.9 %gather_fusion.1 = bf16[12,3,128,128]{3,2,1,0:T(8,128)(2,1)S(1)} fusion(bf16[112,3,128,128]{3,2,1,0:T(8,128)(2,1)} %get-tuple-element.191, s32[1024]{0:T(1024)S(1)} %pad_clamp_fusion.2), kind=kCustom, calls=%fused_computation.1.clone.1 | custom fusion | bytes 2359344 | tf_op jit(solution)/shard_map/while/body/eval_jaxpr/jit(_take)/gather | solution.py:48
  170.9 1.6 fusion.25
  172.7 0.8 constant_dynamic-update-slice_fusion.2
  173.5 0.6 dynamic_slice.25
  175.7 4.9 %gather_fusion.1 = bf16[12,3,128,128]{3,2,1,0:T(8,128)(2,1)S(1)} fusion(bf16[112,3,128,128]{3,2,1,0:T(8,128)(2,1)} %get-tuple-element.191, s32[1024]{0:T(1024)S(1)} %pad_clamp_fusion.2), kind=kCustom, calls=%fused_computation.1.clone.1 | custom fusion | bytes 2359344 | tf_op jit(solution)/shard_map/while/body/eval_jaxpr/jit(_take)/gather | solution.py:48
  181.6 1.6 fusion.25
  183.5 0.9 constant_dynamic-update-slice_fusion.2
  184.3 0.6 dynamic_slice.25
  186.5 4.9 %gather_fusion.1 = bf16[12,3,128,128]{3,2,1,0:T(8,128)(2,1)S(1)} fusion(bf16[112,3,128,128]{3,2,1,0:T(8,128)(2,1)} %get-tuple-element.191, s32[1024]{0:T(1024)S(1)} %pad_clamp_fusion.2), kind=kCustom, calls=%fused_computation.1.clone.1 | custom fusion | bytes 2359344 | tf_op jit(solution)/shard_map/while/body/eval_jaxpr/jit(_take)/gather | solution.py:48
  192.4 1.6 fusion.25
  194.2 0.8 constant_dynamic-update-slice_fusion.2
  195.1 0.6 dynamic_slice.25
  197.3 4.9 %gather_fusion.1 = bf16[12,3,128,128]{3,2,1,0:T(8,128)(2,1)S(1)} fusion(bf16[112,3,128,128]{3,2,1,0:T(8,128)(2,1)} %get-tuple-element.191, s32[1024]{0:T(1024)S(1)} %pad_clamp_fusion.2), kind=kCustom, calls=%fused_computation.1.clone.1 | custom fusion | bytes 2359344 | tf_op jit(solution)/shard_map/while/body/eval_jaxpr/jit(_take)/gather | solution.py:48
  203.2 1.6 fusion.25
  205.0 0.8 constant_dynamic-update-slice_fusion.2
  205.8 0.6 dynamic_slice.25
  208.0 4.9 %gather_fusion.1 = bf16[12,3,128,128]{3,2,1,0:T(8,128)(2,1)S(1)} fusion(bf16[112,3,128,128]{3,2,1,0:T(8,128)(2,1)} %get-tuple-element.191, s32[1024]{0:T(1024)S(1)} %pad_clamp_fusion.2), kind=kCustom, calls=%fused_computation.1.clone.1 | custom fusion | bytes 2359344 | tf_op jit(solution)/shard_map/while/body/eval_jaxpr/jit(_take)/gather | solution.py:48
  213.9 1.6 fusion.25
  215.8 0.8 constant_dynamic-update-slice_fusion.2
  216.6 0.6 dynamic_slice.25
  218.8 4.9 %gather_fusion.1 = bf16[12,3,128,128]{3,2,1,0:T(8,128)(2,1)S(1)} fusion(bf16[112,3,128,128]{3,2,1,0:T(8,128)(2,1)} %get-tuple-element.191, s32[1024]{0:T(1024)S(1)} %pad_clamp_fusion.2), kind=kCustom, calls=%fused_computation.1.clone.1 | custom fusion | bytes 2359344 | tf_op jit(solution)/shard_map/while/body/eval_jaxpr/jit(_take)/gather | solution.py:48
  224.7 1.6 fusion.25
  226.5 0.9 constant_dynamic-update-slice_fusion.2
  227.4 0.6 dynamic_slice.25
  229.6 4.9 %gather_fusion.1 = bf16[12,3,128,128]{3,2,1,0:T(8,128)(2,1)S(1)} fusion(bf16[112,3,128,128]{3,2,1,0:T(8,128)(2,1)} %get-tuple-element.191, s32[1024]{0:T(1024)S(1)} %pad_clamp_fusion.2), kind=kCustom, calls=%fused_computation.1.clone.1 | custom fusion | bytes 2359344 | tf_op jit(solution)/shard_map/while/body/eval_jaxpr/jit(_take)/gather | solution.py:48
  235.5 1.6 fusion.25
  237.3 0.8 constant_dynamic-update-slice_fusion.2
  238.2 116.9 %reduce-scatter.2.cloned.1.call-done = f32[3,4,128,128]{3,2,1,0:T(8,128)} async-done(((f32[24,4,128,128]{3,2,1,0:T(8,128)}), f32[3,4,128,128]{3,2,1,0:T(8,128)}) %reduce-scatter.2.cloned.1.call-update) | async-done | bytes 786448 | tf_op jit(solution)/shard_map/reduce_scatter | solution.py:71
  (203 shorter events, 23.5 us)
Async XLA Ops:
  44.0 2.8 collective-permute-start
  44.0 6.3 %copy-start = (s32[3,8,6]{2,1,0:T(8,128)S(1)}, s32[3,8,6]{2,1,0:T(8,128)}, u32[]{:S(2)}) copy-start(s32[3,8,6]{2,1,0:T(8,128)} %param.8) | copy-start | bytes 1732
  44.0 10.3 %copy-start.2 = (s32[112,1,3]{0,1,2:T(1,128)S(1)}, s32[112,1,3]{0,1,2:T(1,128)}, u32[]{:S(2)}) copy-start(s32[112,1,3]{0,1,2:T(1,128)} %param.10) | copy-start | bytes 4036
  44.0 10.4 %copy-start.1 = (s32[24,1,4]{0,2,1:T(4,128)S(1)}, s32[24,1,4]{0,2,1:T(4,128)}, u32[]{:S(2)}) copy-start(s32[24,1,4]{0,2,1:T(4,128)} %param.11) | copy-start | bytes 1156
  48.8 53.6 %collective-permute-start.1 = (bf16[24,1,6,128,64]{3,4,2,1,0:T(8,128)(2,1)}, bf16[24,1,6,128,64]{3,4,2,1,0:T(8,128)(2,1)}, u32[]{:S(2)}, u32[]{:S(2)}) collective-permute-start(bf16[24,1,6,128,64]{3,4,2,1,0:T(8,128)(2,1)} %maximum_select_fusion.2), channel_id=1, source_target_pairs={{0,2},{1,3},{2,0},{3,1},{4,6},{5,7},{6,4},{7,5},{8,10},{9,11},{10,... | collective-permute-start | bytes 7077896 | tf_op jit(solution)/shard_map/ppermute | solution.py:12
  50.9 9.9 %all-to-all-start = ((s32[3,8,6]{2,0,1:T(4,128)}), s32[3,8,6]{2,0,1:T(4,128)S(1)}, u32[]{:S(2)}, u32[]{:S(2)}) async-start(s32[3,8,6]{2,0,1:T(4,128)} %copy.31), calls=%async_computation | async-start | bytes 32768 | tf_op jit(solution)/shard_map/all_to_all | solution.py:67
  54.3 300.8 %reduce-scatter.2.cloned.1.call-start = ((), (), s32[]{:S(2)}) async-start(), calls=%async_computation.3 | async-start | bytes 7077888 | tf_op jit(solution)/shard_map/reduce_scatter | solution.py:71
Sparse Core Ops, SparseCore 0:
  238.3 116.7 reduce-scatter.1
